TPU v7x, 128 devices: a whole 4x4x4 slice. The times are simulated.
128 devices in a mesh: gx: 8 (over y, core), gy: 16 (over x, z).
Axes of the slice: x: 4, y: 4, z: 4, core: 2. Of those that a mesh axis runs over, the one named last changes fastest.
Arguments:
- cell_state: float32 [16, 1048576], P(None, ('gx', 'gy')), may hold values from -6 to 6
- geometry: float32 [7, 524288], P(None, ('gx', 'gy')), may hold values from -8 to 8, as said below
- surface_cell: int32 [524288], P(('gx', 'gy')), may hold values from 0 to 8191
- counts: int32 [128], P(('gx', 'gy')), may hold values from 128 to 4096, as said below
- wavenumbers: float32 [4], replicated, may hold values from 8 to 24
- target: float32 [4, 2, 2048], replicated, may hold values from -6 to 6
- direction_weight: float32 [2048], replicated, may hold values from 0.3 to 3
Outputs:
- far_field: float32 [4, 2, 2048], replicated
- objective: float32 [], replicated
- cell_adjoint: float32 [16, 1048576], P(None, ('gx', 'gy'))
Inputs may be any that keep to these rules, and one draw needn't show every extreme that they name: Every count is a multiple of 128; one device's count is 4096; all counts together make 128 * 1024. `geometry`: rows 3 to 5 are unit vectors; row 6 is positive.
All inputs are finite; a program needn't handle non-finite values.
Results may differ from a plain program's by a relative error of at most 0.022.
Values sent between devices are 32-bit elements; how exact they have to be, the bound alone decides.
A program may use at most 128 MiB of HBM per device.

v0:
```python
import math
import jax
import jax.numpy as jnp
from jax import lax
from jax.sharding import PartitionSpec as P

GOLDEN = math.pi * (3.0 - math.sqrt(5.0))


def directions(count_dirs):
    lattice = jnp.arange(count_dirs).astype(jnp.float32)
    height = 1.0 - (2.0 * lattice + 1.0) / count_dirs
    radius_xy = jnp.sqrt(1.0 - height * height)
    azimuth = jnp.mod(lattice * GOLDEN, 2.0 * math.pi)
    return (radius_xy * jnp.cos(azimuth), radius_xy * jnp.sin(azimuth), height)


def kernel_block(points, wavenum, east_x, north_y, upward):
    phases = wavenum * (
        points[0][:, None] * east_x[None, :]
        + points[1][:, None] * north_y[None, :]
        + points[2][:, None] * upward[None, :]
    )
    return jnp.concatenate([jnp.cos(phases), jnp.sin(phases)], axis=1).astype(jnp.bfloat16)


def source_rows(rows_block, level):
    surface_area = rows_block[22]
    normal = rows_block[19:22]
    pressure_real = rows_block[level] * surface_area
    pressure_imag = rows_block[4 + level] * surface_area
    return jnp.stack(
        [
            rows_block[8 + level] * surface_area,
            normal[0] * pressure_real,
            normal[1] * pressure_real,
            normal[2] * pressure_real,
            rows_block[12 + level] * surface_area,
            normal[0] * pressure_imag,
            normal[1] * pressure_imag,
            normal[2] * pressure_imag,
        ]
    ).astype(jnp.bfloat16)


def far_field_of(sums, wavenumbers, direction_basis):
    half_width = sums.shape[2] // 2
    cosine_part = sums[:, :, :half_width]
    sine_part = sums[:, :, half_width:]
    real_q = cosine_part[:, 0:4] + sine_part[:, 4:8]
    imag_q = cosine_part[:, 4:8] - sine_part[:, 0:4]
    real_z = jnp.sum(direction_basis[None] * real_q, axis=1)
    imag_z = jnp.sum(direction_basis[None] * imag_q, axis=1)
    wavenum = wavenumbers[:, None]
    return jnp.stack([-wavenum * imag_z, wavenum * real_z], axis=1)


def adjoint_weights(far_field, target, direction_weight, wavenumbers, direction_basis):
    count_dirs = far_field.shape[2]
    mismatch = far_field - target
    objective = jnp.sum(direction_weight * mismatch * mismatch) / count_dirs
    gradient = 2.0 * direction_weight * mismatch / count_dirs
    wavenum = wavenumbers[:, None]
    real_gz = wavenum * gradient[:, 1]
    imag_gz = -wavenum * gradient[:, 0]
    real_gq = direction_basis[None] * real_gz[:, None]
    imag_gq = direction_basis[None] * imag_gz[:, None]
    upper_half = jnp.concatenate([real_gq, -imag_gq], axis=2)
    lower_half = jnp.concatenate([imag_gq, real_gq], axis=2)
    return (objective, jnp.concatenate([upper_half, lower_half], axis=1).astype(jnp.bfloat16))


def adjoint_sources(products, normal):
    pressure_real = jnp.sum(normal[None] * products[:, 1:4], axis=1)
    pressure_imag = jnp.sum(normal[None] * products[:, 5:8], axis=1)
    return jnp.concatenate([pressure_real, pressure_imag, products[:, 0], products[:, 4]], axis=0)


def on_device(cell_state, geometry, surface_cell, counts, wavenumbers, target, direction_weight):
    owners = lax.axis_size(("gx", "gy"))
    rows_dev = surface_cell.shape[0]
    capacity = rows_dev // owners
    live_own = rows_dev // 4
    count_dirs = target.shape[2]
    num_freqs = wavenumbers.shape[0]
    living = (jnp.arange(rows_dev) < counts[0]).astype(jnp.float32)
    outgoing = (
        jnp.concatenate(
            [cell_state[:, surface_cell], geometry, jnp.ones((1, rows_dev), jnp.float32)], axis=0
        )
        * living[None, :]
    )
    outgoing = outgoing.reshape(24, capacity, owners)
    arrived = lax.all_to_all(outgoing, ("gx", "gy"), split_axis=2, concat_axis=2, tiled=True)
    marker = arrived[23]
    per_source = jnp.sum(marker, axis=0).astype(jnp.int32)
    offset = jnp.cumsum(per_source) - per_source
    position = offset[None, :] + jnp.arange(capacity, dtype=jnp.int32)[:, None]
    packed_slot = jnp.where(marker > 0.5, position, live_own).reshape(capacity * owners)
    compact = (
        jnp.zeros((23, live_own), jnp.float32)
        .at[:, packed_slot]
        .set(arrived[:23].reshape(23, capacity * owners), mode="drop")
    )
    block_rows = math.gcd(live_own, 1024)
    block_count = live_own // block_rows
    blocks = compact.reshape(23, block_count, block_rows).transpose(1, 0, 2)
    east_x, north_y, upward = directions(count_dirs)
    direction_basis = jnp.stack([jnp.ones_like(east_x), east_x, north_y, upward])

    def forward_block(running, rows_block):
        products = [
            jnp.dot(
                source_rows(rows_block, level),
                kernel_block(rows_block[16:19], wavenumbers[level], east_x, north_y, upward),
                preferred_element_type=jnp.float32,
            )
            for level in range(num_freqs)
        ]
        return (running + jnp.stack(products), None)

    sums, _ = lax.scan(
        forward_block, jnp.zeros((num_freqs, 8, 2 * count_dirs), jnp.float32), blocks
    )
    far_field = lax.psum(far_field_of(sums, wavenumbers, direction_basis), ("gx", "gy"))
    objective, weights = adjoint_weights(
        far_field, target, direction_weight, wavenumbers, direction_basis
    )

    def adjoint_block(carry, rows_block):
        products = [
            lax.dot_general(
                weights[level],
                kernel_block(rows_block[16:19], wavenumbers[level], east_x, north_y, upward),
                (((1,), (1,)), ((), ())),
                preferred_element_type=jnp.float32,
            )
            for level in range(num_freqs)
        ]
        return (carry, adjoint_sources(jnp.stack(products), rows_block[19:22]))

    _, backward = lax.scan(adjoint_block, jnp.zeros((), jnp.float32), blocks)
    backward = backward.transpose(1, 0, 2).reshape(16, live_own)
    spread = backward[:, jnp.minimum(packed_slot, live_own - 1)] * marker.reshape(
        1, capacity * owners
    )
    spread = spread.reshape(16, capacity, owners)
    returned = lax.all_to_all(spread, ("gx", "gy"), split_axis=2, concat_axis=2, tiled=True)
    per_row = returned.reshape(16, rows_dev) * living[None, :]
    cell_adjoint = jnp.zeros(cell_state.shape, jnp.float32).at[:, surface_cell].add(per_row)
    return (far_field, objective, cell_adjoint)


def solution(mesh):
    placed = (
        P(None, ("gx", "gy")),
        P(None, ("gx", "gy")),
        P(("gx", "gy")),
        P(("gx", "gy")),
        P(),
        P(),
        P(),
    )
    return jax.shard_map(
        on_device,
        mesh=mesh,
        in_specs=placed,
        out_specs=(P(), P(), P(None, ("gx", "gy"))),
        check_vma=False,
    )
```

profile of v0, /device:TPU:1, one launch (start us, length us, event | category | flops | bytes accessed | tf_op | source)
XLA Modules:
  0.0 461.3 jit_solution(930296876396630908)
XLA Ops:
  10.5 3.5 copy.346
  14.0 12.9 %gather_fusion = f32[4096,16]{1,0:T(8,128)S(1)} fusion(f32[16,8192]{0,1:T(8,128)} %copy.346, s32[4096]{0:T(1024)S(1)} %get-tuple-element.118), kind=kCustom, calls=%fused_computation | custom fusion | bytes 540672 | tf_op jit(solution)/shard_map/gather | solution.py:89
  28.1 1.3 fusion.51
  29.4 1.4 reshape.322
  30.8 11.5 %all-to-all-start = ((f32[128,1,768]{2,1,0:T(1,128)}), f32[128,1,768]{2,1,0:T(1,128)S(1)}, u32[]{:S(2)}, u32[]{:S(2)}) async-start(f32[128,1,768]{2,1,0:T(1,128)} %reshape.322), calls=%async_computation | async-start | bytes 786432 | tf_op jit(solution)/shard_map/all_to_all | solution.py:94
  43.5 11.0 %all-to-all-done = f32[128,1,768]{2,1,0:T(1,128)S(1)} async-done(((f32[128,1,768]{2,1,0:T(1,128)}), f32[128,1,768]{2,1,0:T(1,128)S(1)}, u32[]{:S(2)}, u32[]{:S(2)}) %all-to-all-start) | async-done | bytes 393248 | tf_op jit(solution)/shard_map/all_to_all | solution.py:94
  55.0 1.5 reduce.8
  59.9 11.2 %scatter_custom_fusion = f32[23,1024]{0,1:T(8,128)S(1)} fusion(s32[4096]{0:T(1024)S(1)} %bitcast.117, f32[4096,23]{1,0:T(8,128)S(1)} %copy.352, f32[]{:T(128)} %constant.23.clone.1), kind=kCustom, calls=%fused_computation.48 | custom fusion | bytes 94212 | tf_op jit(solution)/shard_map/scatter | solution.py:103
  71.1 1.4 slice_reduce_fusion.2
  72.6 5.4 %fusion.49 = (f32[1,1024]{0,1:T(8,128)}, f32[1,1024]{0,1:T(8,128)}, f32[1,1024]{0,1:T(8,128)}, f32[1,1024]{0,1:T(8,128)}, f32[1,1024]{0,1:T(8,128)}, /*index=5*/...) fusion(f32[23,1024]{0,1:T(8,128)S(1)} %scatter_custom_fusion), kind=kLoop, calls=%fused_computation.158 | loop fusion | bytes 155648 | tf_op jit(solution)/shard_map/while/body/eval_jaxpr/slice | solution.py:31
  81.7 1.2 copy.401
  82.9 1.2 copy.400
  84.2 1.2 copy.399
  89.1 1.2 copy.395
  90.3 1.2 copy.394
  91.6 1.2 copy.393
  97.7 126.3 %cosine_convert_fusion.3 = (bf16[1024,2048]{1,0:T(8,128)(2,1)S(1)}, bf16[1024,2048]{1,0:T(8,128)(2,1)}, bf16[1024,2048]{1,0:T(8,128)(2,1)}, bf16[1024,2048]{1,0:...) fusion(f32[2048]{0:T(1024)S(1)} %multiply_subtract_fusion, ...), kind=kLoop, calls=%fused_computation.15 | loop fusion | flops 35651584 | bytes 33591312 | tf_op jit(solution)/shard_map/convert.36
  226.0 1.3 copy-done.2
  227.4 4.1 fusion.14
  231.6 4.1 fusion.13
  235.8 4.3 fusion.15
  241.6 133.9 %all-reduce.2.cloned.1.call-done = f32[4,2,2048]{2,0,1:T(4,128)} async-done(((f32[4,2,2048]{2,0,1:T(4,128)}), f32[4,2,2048]{2,0,1:T(4,128)}) %all-reduce.2.cloned.1.call-update) | async-done | bytes 65552 | tf_op jit(solution)/shard_map/psum | solution.py:125
  375.5 1.5 multiply_multiply_fusion.1
  377.3 4.8 %fusion.21 = f32[1,8,1024]{2,1,0:T(8,128)S(1)} fusion(bf16[1024,2048]{1,0:T(8,128)(2,1)} %get-tuple-element.112, bf16[1024,2048]{1,0:T(8,128)(2,1)} %get-tuple-element.113, bf16[4,8,4096]{2,1,0:T(8,128)(2,1)S(1)} %maximum_maximum_fusion), kind=kOutput, calls=%fused_computation.39 | convolution fusion | flops 83886080 | bytes 8486912 | tf_op jit(solution)/shard_map/while/body/eval_jaxpr/dot_general | solution.py:132
  383.2 2.3 fusion.20
  386.7 2.3 fusion.19
  390.2 2.3 fusion.18
  392.9 10.8 %gather_fusion.1 = f32[4096,16]{1,0:T(8,128)S(1)} fusion(f32[16,1024]{0,1:T(8,128)S(1)} %copy.376, s32[4096]{0:T(1024)S(1)} %broadcast_clamp_fusion), kind=kCustom, calls=%fused_computation.1 | custom fusion | bytes 540672 | tf_op jit(solution)/shard_map/gather | solution.py:144
  406.0 5.4 %all-to-all-start.1 = ((f32[128,1,512]{2,1,0:T(1,128)}), f32[128,1,512]{2,1,0:T(1,128)S(1)}, u32[]{:S(2)}, u32[]{:S(2)}) async-start(f32[128,1,512]{2,1,0:T(1,128)} %reshape.324), calls=%async_computation.1 | async-start | bytes 524288 | tf_op jit(solution)/shard_map/all_to_all | solution.py:148
  412.8 9.7 %all-to-all-done.1 = f32[128,1,512]{2,1,0:T(1,128)S(1)} async-done(((f32[128,1,512]{2,1,0:T(1,128)}), f32[128,1,512]{2,1,0:T(1,128)S(1)}, u32[]{:S(2)}, u32[]{:S(2)}) %all-to-all-start.1) | async-done | bytes 262176 | tf_op jit(solution)/shard_map/all_to_all | solution.py:148
  425.1 24.5 %scatter_custom_fusion.1 = f32[16,8192]{0,1:T(8,128)} fusion(s32[4096]{0:T(1024)S(1)} %get-tuple-element.117, f32[4096,16]{1,0:T(8,128)S(1)} %copy.380, f32[]{:T(128)} %constant.23.clone.1), kind=kCustom, calls=%fused_computation.33 | custom fusion | flops 65536 | bytes 524292 | tf_op jit(solution)/shard_map/scatter-add | solution.py:150
  449.6 3.5 copy.382
  (105 shorter events, 34.5 us)
Async XLA Ops:
  26.9 15.8 %copy-start.11 = (f32[4]{0:T(128)S(1)}, f32[4]{0:T(128)}, u32[]{:S(2)}) copy-start(f32[4]{0:T(128)} %param.11) | copy-start | bytes 52
  26.9 16.4 %copy-start.10 = (f32[2048]{0:T(1024)S(1)}, f32[2048]{0:T(1024)}, u32[]{:S(2)}) copy-start(f32[2048]{0:T(1024)} %param.13) | copy-start | bytes 24580
  30.8 23.6 %all-to-all-start = ((f32[128,1,768]{2,1,0:T(1,128)}), f32[128,1,768]{2,1,0:T(1,128)S(1)}, u32[]{:S(2)}, u32[]{:S(2)}) async-start(f32[128,1,768]{2,1,0:T(1,128)} %reshape.322), calls=%async_computation | async-start | bytes 786432 | tf_op jit(solution)/shard_map/all_to_all | solution.py:94
  42.3 333.1 %all-reduce.2.cloned.1.call-start = ((), (), s32[]{:S(2)}) async-start(), calls=%async_computation.2 | async-start | bytes 131072 | tf_op jit(solution)/shard_map/psum | solution.py:125
  224.0 1.9 copy-start
  224.0 3.3 copy-start.2
  235.8 139.7 %copy-start.9 = (f32[4,2,2048]{2,1,0:T(2,128)S(1)}, f32[4,2,2048]{2,1,0:T(2,128)}, u32[]{:S(2)}) copy-start(f32[4,2,2048]{2,1,0:T(2,128)} %param.12) | copy-start | bytes 196612
  377.3 4.8 %copy-start.6 = (bf16[1024,2048]{1,0:T(8,128)(2,1)S(1)}, bf16[1024,2048]{1,0:T(8,128)(2,1)}, u32[]{:S(2)}) copy-start(bf16[1024,2048]{1,0:T(8,128)(2,1)} %get-tuple-element.107) | copy-start | bytes 12582916
  377.3 5.9 %copy-start.7 = (bf16[1024,2048]{1,0:T(8,128)(2,1)S(1)}, bf16[1024,2048]{1,0:T(8,128)(2,1)}, u32[]{:S(2)}) copy-start(bf16[1024,2048]{1,0:T(8,128)(2,1)} %get-tuple-element.111) | copy-start | bytes 12582916
  383.2 2.3 copy-start.4
  383.2 3.5 copy-start.5
  386.7 2.3 copy-start.1
  386.7 3.5 copy-start.3
  392.8 19.2 %copy-start.8 = (f32[4,2,2048]{2,0,1:T(4,128)S(1)}, f32[4,2,2048]{2,0,1:T(4,128)}, u32[]{:S(2)}) copy-start(f32[4,2,2048]{2,0,1:T(4,128)} %all-reduce.2.cloned.1.call-done) | copy-start | bytes 196612
  406.0 16.5 %all-to-all-start.1 = ((f32[128,1,512]{2,1,0:T(1,128)}), f32[128,1,512]{2,1,0:T(1,128)S(1)}, u32[]{:S(2)}, u32[]{:S(2)}) async-start(f32[128,1,512]{2,1,0:T(1,128)} %reshape.324), calls=%async_computation.1 | async-start | bytes 524288 | tf_op jit(solution)/shard_map/all_to_all | solution.py:148
Sparse Core Ops, SparseCore 0:
  241.3 134.1 all-reduce.1
where the time goes:
time: 469 us; the launch traced here: 461 us
  other arithmetic  161 us (34%)
  waiting for transfers between devices  155 us (33%)
  local copies, waits for them, and re-layouts  86.5 us (18%)
  matrix products  25.3 us (5%)
  between operations  17.1 us (4%)
  starting transfers between devices  17 us (4%)
    psum x1, waiting for transfers between devices, on_device(): lax.psum(far_field_of(sums, wavenumbers, direction_basis), ('gx', 'gy'))  134 us
    another operation x6, other arithmetic  127 us
    unnamed x57, local copies, waits for them, and re-layouts  37.4 us
    scatter-add x1, other arithmetic, on_device(): jnp.zeros(cell_state.shape, jnp.float32).at[:, surface_cell].add(per_row)  24.5 us
    dot_general x4, matrix products, forward_block(): jnp.dot(source_rows(rows_block, level), kernel_block(rows_block[16:19], w...  13.8 us
    gather x1, local copies, waits for them, and re-layouts, on_device(): cell_state[:, surface_cell]  12.9 us
    gather x2, local copies, waits for them, and re-layouts, on_device(): backward[:, jnp.minimum(packed_slot, live_own - 1)]  11.8 us
    dot_general x4, matrix products, adjoint_block(): lax.dot_general(weights[level], kernel_block(rows_block[16:19], wavenumbe...  11.6 us
  transfers between devices with their start and end apart: 3, of which 3 were waited for; matrix products, arithmetic and copies ran while one was open for 0% of the time, Pallas kernels for 0%

commit v1 on v0

--- a/solution.py
+++ b/solution.py
@@ -122,7 +122,9 @@
     sums, _ = lax.scan(
         forward_block, jnp.zeros((num_freqs, 8, 2 * count_dirs), jnp.float32), blocks
     )
-    far_field = lax.psum(far_field_of(sums, wavenumbers, direction_basis), ("gx", "gy"))
+    own = far_field_of(sums, wavenumbers, direction_basis)
+    parts = lax.all_gather(own, ("gx", "gy"), axis=0, tiled=False)
+    far_field = parts.sum(axis=0)
     objective, weights = adjoint_weights(
         far_field, target, direction_weight, wavenumbers, direction_basis
     )

time: 469 us -> 415 us (0.88)
  waiting for transfers between devices: 155 us -> 87.8 us
  local copies, waits for them, and re-layouts: 86.5 us -> 93.5 us
  other arithmetic: 161 us -> 166 us
    psum x1 -> x0, waiting for transfers between devices: 134 us -> none  [on_device(): lax.psum(far_field_of(sums, wavenumbers, direction_basis), ('gx', 'gy'))]
    all_gather x0 -> x1, waiting for transfers between devices: none -> 66.6 us  [on_device(): parts = lax.all_gather(own, ('gx', 'gy'), axis=0, tiled=False)]
    reduce_sum x0 -> x1, other arithmetic: none -> 6.91 us  [on_device(): far_field = parts.sum(axis=0)]
    gather x2, local copies, waits for them, and re-layouts: 11.8 us -> 16.8 us  [on_device(): backward[:, jnp.minimum(packed_slot, live_own - 1)]]
    unnamed x57 -> x58, local copies, waits for them, and re-layouts: 37.4 us -> 35.6 us
where the time goes in v1:
time: 415 us; the launch traced here: 407 us
  other arithmetic  166 us (40%)
  local copies, waits for them, and re-layouts  93.5 us (23%)
  waiting for transfers between devices  87.8 us (21%)
  matrix products  25.7 us (6%)
  between operations  17.3 us (4%)
  starting transfers between devices  16.9 us (4%)
    another operation x6, other arithmetic  127 us
    all_gather x1, waiting for transfers between devices, on_device(): parts = lax.all_gather(own, ('gx', 'gy'), axis=0, tiled=False)  66.6 us
    unnamed x58, local copies, waits for them, and re-layouts  35.6 us
    scatter-add x1, other arithmetic, on_device(): jnp.zeros(cell_state.shape, jnp.float32).at[:, surface_cell].add(per_row)  24.5 us
    gather x2, local copies, waits for them, and re-layouts, on_device(): backward[:, jnp.minimum(packed_slot, live_own - 1)]  16.8 us
    gather x1, local copies, waits for them, and re-layouts, on_device(): cell_state[:, surface_cell]  16.3 us
    dot_general x4, matrix products, forward_block(): jnp.dot(source_rows(rows_block, level), kernel_block(rows_block[16:19], w...  13.8 us
    dot_general x4, matrix products, adjoint_block(): lax.dot_general(weights[level], kernel_block(rows_block[16:19], wavenumbe...  12 us
  transfers between devices with their start and end apart: 3, of which 3 were waited for; matrix products, arithmetic and copies ran while one was open for 0% of the time, Pallas kernels for 0%

profile of v1, /device:TPU:1, one launch (start us, length us, event | category | flops | bytes accessed | tf_op | source)
XLA Modules:
  0.0 407.3 jit_solution(16268694652465154338)
XLA Ops:
  9.7 3.5 copy.348
  13.2 16.3 %gather_fusion = f32[4096,16]{1,0:T(8,128)} fusion(f32[16,8192]{0,1:T(8,128)} %copy.348, s32[4096]{0:T(1024)S(1)} %get-tuple-element.118), kind=kCustom, calls=%fused_computation | custom fusion | bytes 540672 | tf_op jit(solution)/shard_map/gather | solution.py:89
  29.5 2.5 copy.349
  32.3 1.4 reshape.323
  33.8 11.5 %all-to-all-start = ((f32[128,1,768]{2,1,0:T(1,128)}), f32[128,1,768]{2,1,0:T(1,128)S(1)}, u32[]{:S(2)}, u32[]{:S(2)}) async-start(f32[128,1,768]{2,1,0:T(1,128)} %reshape.323), calls=%async_computation | async-start | bytes 786432 | tf_op jit(solution)/shard_map/all_to_all | solution.py:94
  46.5 10.9 %all-to-all-done = f32[128,1,768]{2,1,0:T(1,128)S(1)} async-done(((f32[128,1,768]{2,1,0:T(1,128)}), f32[128,1,768]{2,1,0:T(1,128)S(1)}, u32[]{:S(2)}, u32[]{:S(2)}) %all-to-all-start) | async-done | bytes 393248 | tf_op jit(solution)/shard_map/all_to_all | solution.py:94
  57.9 1.5 reduce.8
  62.8 10.9 %scatter_custom_fusion = f32[23,1024]{0,1:T(8,128)S(1)} fusion(s32[4096]{0:T(1024)S(1)} %bitcast.123, f32[4096,23]{1,0:T(8,128)S(1)} %copy.354, f32[]{:T(128)} %constant.23.clone.1), kind=kCustom, calls=%fused_computation.48 | custom fusion | bytes 94212 | tf_op jit(solution)/shard_map/scatter | solution.py:103
  73.8 1.4 slice_reduce_fusion.2
  75.2 5.4 %fusion.47 = (f32[1,1024]{0,1:T(8,128)}, f32[1,1024]{0,1:T(8,128)}, f32[1,1024]{0,1:T(8,128)}, f32[1,1024]{0,1:T(8,128)}, f32[1,1024]{0,1:T(8,128)}, /*index=5*/...) fusion(f32[23,1024]{0,1:T(8,128)S(1)} %scatter_custom_fusion), kind=kLoop, calls=%fused_computation.157 | loop fusion | bytes 155648 | tf_op jit(solution)/shard_map/while/body/eval_jaxpr/slice | solution.py:31
  85.6 1.2 copy.404
  86.8 1.2 copy.403
  88.0 1.2 copy.402
  89.3 1.2 copy.401
  94.2 1.2 copy.397
  100.4 126.4 %cosine_convert_fusion.3 = (bf16[1024,2048]{1,0:T(8,128)(2,1)S(1)}, bf16[1024,2048]{1,0:T(8,128)(2,1)}, bf16[1024,2048]{1,0:T(8,128)(2,1)}, bf16[1024,2048]{1,0:...) fusion(f32[2048]{0:T(1024)S(1)} %multiply_subtract_fusion, ...), kind=kLoop, calls=%fused_computation.15 | loop fusion | flops 35651584 | bytes 33591312 | tf_op jit(solution)/shard_map/convert.36
  226.7 1.9 copy-done
  230.1 4.1 %fusion.14 = f32[1,8,4096]{2,1,0:T(8,128)S(1)} fusion(bf16[8,1024]{1,0:T(8,128)(2,1)S(1)} %stack.140, bf16[1024,2048]{1,0:T(8,128)(2,1)} %get-tuple-element.111, bf16[1024,2048]{1,0:T(8,128)(2,1)} %get-tuple-element.107), kind=kOutput, calls=%fused_computation.31 | convolution fusion | flops 83886080 | bytes 8536064 | tf_op jit(solution)/shard_map/while/body/eval_jaxpr/dot_general | solution.py:113
  234.3 4.1 %fusion.13 = f32[1,8,4096]{2,1,0:T(8,128)S(1)} fusion(bf16[8,1024]{1,0:T(8,128)(2,1)S(1)} %stack.138, bf16[1024,2048]{1,0:T(8,128)(2,1)} %get-tuple-element.110, bf16[1024,2048]{1,0:T(8,128)(2,1)} %get-tuple-element.108), kind=kOutput, calls=%fused_computation.30 | convolution fusion | flops 83886080 | bytes 8536064 | tf_op jit(solution)/shard_map/while/body/eval_jaxpr/dot_general | solution.py:113
  238.5 4.3 %fusion.15 = f32[1,8,4096]{2,1,0:T(8,128)S(1)} fusion(bf16[8,1024]{1,0:T(8,128)(2,1)S(1)} %stack.142, bf16[1024,2048]{1,0:T(8,128)(2,1)} %get-tuple-element.112, bf16[1024,2048]{1,0:T(8,128)(2,1)} %get-tuple-element.113), kind=kOutput, calls=%fused_computation.32 | convolution fusion | flops 83886080 | bytes 8536064 | tf_op jit(solution)/shard_map/while/body/eval_jaxpr/dot_general | solution.py:113
  244.4 66.6 %all-gather.3.cloned.1.call-done = f32[512,2,2048]{2,1,0:T(2,128)} async-done(((f32[4,2,2048]{2,1,0:T(2,128)}), f32[512,2,2048]{2,1,0:T(2,128)}) %all-gather.3.cloned.1.call-update) | async-done | bytes 8388624 | tf_op jit(solution)/shard_map/all_gather | solution.py:126
  311.1 6.9 %reduce_sum.74 = f32[4,2,2048]{2,1,0:T(2,128)S(1)} reduce(f32[128,4,2,2048]{3,2,1,0:T(2,128)} %bitcast.103, f32[]{:T(128)} %constant.23.clone.1), dimensions={0}, to_apply=%region_5.6 | reduce | flops 2080768 | bytes 8454148 | tf_op jit(solution)/shard_map/reduce_sum | solution.py:127
  319.1 5.2 %fusion.21 = f32[1,8,1024]{2,1,0:T(8,128)S(1)} fusion(bf16[1024,2048]{1,0:T(8,128)(2,1)} %get-tuple-element.112, bf16[1024,2048]{1,0:T(8,128)(2,1)} %get-tuple-element.113, bf16[4,8,4096]{2,1,0:T(8,128)(2,1)S(1)} %maximum_maximum_fusion), kind=kOutput, calls=%fused_computation.39 | convolution fusion | flops 83886080 | bytes 8486912 | tf_op jit(solution)/shard_map/while/body/eval_jaxpr/dot_general | solution.py:134
  324.3 2.3 fusion.20
  327.8 2.3 fusion.19
  331.2 2.3 fusion.18
  333.9 14.3 %gather_fusion.1 = f32[4096,16]{1,0:T(8,128)} fusion(f32[16,1024]{0,1:T(8,128)S(1)} %copy.379, s32[4096]{0:T(1024)S(1)} %broadcast_clamp_fusion), kind=kCustom, calls=%fused_computation.1 | custom fusion | bytes 540672 | tf_op jit(solution)/shard_map/gather | solution.py:146
  348.2 2.5 copy.381
  352.0 5.3 %all-to-all-start.1 = ((f32[128,1,512]{2,1,0:T(1,128)}), f32[128,1,512]{2,1,0:T(1,128)S(1)}, u32[]{:S(2)}, u32[]{:S(2)}) async-start(f32[128,1,512]{2,1,0:T(1,128)} %reshape.325), calls=%async_computation.1 | async-start | bytes 524288 | tf_op jit(solution)/shard_map/all_to_all | solution.py:150
  358.0 10.2 %all-to-all-done.1 = f32[128,1,512]{2,1,0:T(1,128)S(1)} async-done(((f32[128,1,512]{2,1,0:T(1,128)}), f32[128,1,512]{2,1,0:T(1,128)S(1)}, u32[]{:S(2)}, u32[]{:S(2)}) %all-to-all-start.1) | async-done | bytes 262176 | tf_op jit(solution)/shard_map/all_to_all | solution.py:150
  370.8 24.5 %scatter_custom_fusion.1 = f32[16,8192]{0,1:T(8,128)} fusion(s32[4096]{0:T(1024)S(1)} %get-tuple-element.117, f32[4096,16]{1,0:T(8,128)S(1)} %copy.383, f32[]{:T(128)} %constant.23.clone.1), kind=kCustom, calls=%fused_computation.33 | custom fusion | flops 65536 | bytes 524292 | tf_op jit(solution)/shard_map/scatter-add | solution.py:152
  395.3 3.5 copy.384
  (107 shorter events, 31.6 us)
Async XLA Ops:
  9.5 36.2 %copy-start.11 = (f32[4]{0:T(128)S(1)}, f32[4]{0:T(128)}, u32[]{:S(2)}) copy-start(f32[4]{0:T(128)} %param.11) | copy-start | bytes 52
  33.8 23.6 %all-to-all-start = ((f32[128,1,768]{2,1,0:T(1,128)}), f32[128,1,768]{2,1,0:T(1,128)S(1)}, u32[]{:S(2)}, u32[]{:S(2)}) async-start(f32[128,1,768]{2,1,0:T(1,128)} %reshape.323), calls=%async_computation | async-start | bytes 786432 | tf_op jit(solution)/shard_map/all_to_all | solution.py:94
  45.3 265.8 %all-gather.3.cloned.1.call-start = ((), (), s32[]{:S(2)}) async-start(), calls=%async_computation.2 | async-start | bytes 8454144 | tf_op jit(solution)/shard_map/all_gather | solution.py:126
  226.7 1.9 copy-start
  226.7 3.3 copy-start.2
  238.4 5.6 %copy-start.10 = (f32[2048]{0:T(1024)S(1)}, f32[2048]{0:T(1024)}, u32[]{:S(2)}) copy-start(f32[2048]{0:T(1024)} %param.13) | copy-start | bytes 24580
  242.8 75.2 %copy-start.9 = (f32[4,2,2048]{2,1,0:T(2,128)S(1)}, f32[4,2,2048]{2,1,0:T(2,128)}, u32[]{:S(2)}) copy-start(f32[4,2,2048]{2,1,0:T(2,128)} %param.12) | copy-start | bytes 196612
  318.0 8.6 %copy-start.8 = (f32[4,2,2048]{2,1,0:T(2,128)}, f32[4,2,2048]{2,1,0:T(2,128)S(1)}, u32[]{:S(2)}) copy-start(f32[4,2,2048]{2,1,0:T(2,128)S(1)} %reduce_sum.74) | copy-start | bytes 196612
  318.0 6.3 %copy-start.6 = (bf16[1024,2048]{1,0:T(8,128)(2,1)S(1)}, bf16[1024,2048]{1,0:T(8,128)(2,1)}, u32[]{:S(2)}) copy-start(bf16[1024,2048]{1,0:T(8,128)(2,1)} %get-tuple-element.107) | copy-start | bytes 12582916
  318.0 6.3 %copy-start.7 = (bf16[1024,2048]{1,0:T(8,128)(2,1)S(1)}, bf16[1024,2048]{1,0:T(8,128)(2,1)}, u32[]{:S(2)}) copy-start(bf16[1024,2048]{1,0:T(8,128)(2,1)} %get-tuple-element.111) | copy-start | bytes 12582916
  324.3 2.3 copy-start.4
  324.3 3.5 copy-start.5
  327.8 2.3 copy-start.1
  327.8 3.5 copy-start.3
  352.0 16.2 %all-to-all-start.1 = ((f32[128,1,512]{2,1,0:T(1,128)}), f32[128,1,512]{2,1,0:T(1,128)S(1)}, u32[]{:S(2)}, u32[]{:S(2)}) async-start(f32[128,1,512]{2,1,0:T(1,128)} %reshape.325), calls=%async_computation.1 | async-start | bytes 524288 | tf_op jit(solution)/shard_map/all_to_all | solution.py:150
Sparse Core Ops, SparseCore 0:
  244.1 66.8 all-gather.2
